TPU v7x, 32 devices: a whole 2x2x4 slice. The times are simulated.
32 devices in a mesh: dp: 8 (over z, x), fsdp: 4 (over y, core).
Axes of the slice: x: 2, y: 2, z: 4, core: 2. Of those that a mesh axis runs over, the one named last changes fastest.
Arguments:
- hidden_in: float32 [32, 496, 768], P(('dp', 'fsdp')), may hold values from -6 to 6
- cotangent: float32 [32, 496, 768], P(('dp', 'fsdp')), may hold values from -6 to 6
- lengths: int32 [32], P(('dp', 'fsdp')), may hold values from 397 to 496, as said below
- qkv_weight: float32 [2, 768, 2304], P(None, ('dp', 'fsdp')), may hold values from -0.21875 to 0.21875
- out_weight: float32 [2, 768, 768], P(None, ('dp', 'fsdp')), may hold values from -6 to 6
- up_weight: float32 [2, 768, 3072], P(None, ('dp', 'fsdp')), may hold values from -0.21875 to 0.21875
- down_weight: float32 [2, 3072, 768], P(None, None, ('dp', 'fsdp')), may hold values from -0.109375 to 0.109375
- norm_gains: float32 [2, 2, 768], P(None, None, ('dp', 'fsdp')), may hold values from 0.5 to 1.5
- biases: float32 [2, 6, 768], P(None, None, ('dp', 'fsdp')), may hold values from -1.2 to 1.2
- up_bias: float32 [2, 3072], P(None, ('dp', 'fsdp')), may hold values from -1.2 to 1.2
Outputs:
- output: float32 [32, 496, 768], P(('dp', 'fsdp'))
- input_grad: float32 [32, 496, 768], P(('dp', 'fsdp'))
- qkv_grad: float32 [2, 768, 2304], P(None, ('dp', 'fsdp'))
- out_grad: float32 [2, 768, 768], P(None, ('dp', 'fsdp'))
- up_grad: float32 [2, 768, 3072], P(None, ('dp', 'fsdp'))
- down_grad: float32 [2, 3072, 768], P(None, None, ('dp', 'fsdp'))
- gains_grad: float32 [2, 2, 768], P(None, None, ('dp', 'fsdp'))
- biases_grad: float32 [2, 6, 768], P(None, None, ('dp', 'fsdp'))
- up_bias_grad: float32 [2, 3072], P(None, ('dp', 'fsdp'))
Inputs may be any that keep to these rules, and one draw needn't show every extreme that they name: `lengths`: valid patches of each clip; some clip has exactly 496.
All inputs are finite; a program needn't handle non-finite values.
Results may differ from a plain program's by a relative error of at most 0.013.
Values may be sent and summed in bfloat16 or wider, within the bound.
No kernel may reach another device: no remote copies, remote signals or barrier semaphores. Data moves between devices by JAX's collectives and lax.ppermute only.
A program may use at most 320 MiB of HBM per device.

v0:
```python
import jax
import jax.numpy as jnp
from jax import lax
from jax.sharding import PartitionSpec as P

HEADS = 12
HEAD_WIDTH = 64
norm_eps = 1e-06
section_kinds = ("rows", "rows", "rows", "cols", "cols", "flat", "cols")


def layer_norm(values, gain, shift):
    center = values - jnp.mean(values, axis=-1, keepdims=True)
    spread = jnp.mean(center * center, axis=-1, keepdims=True)
    return center * lax.rsqrt(spread + norm_eps) * gain + shift


def gelu_exact(values):
    return jax.nn.gelu(values, approximate=False)


def pack_owned(pieces):
    return jnp.concatenate([piece.reshape(1, -1) for piece in pieces], axis=1)


def unpack_whole(gathered, shapes):
    count = gathered.shape[0]
    result = []
    offset = 0
    for shape, kind in zip(shapes, section_kinds):
        length = 1
        for extent in shape:
            length = length * extent
        section = gathered[:, offset : offset + length]
        offset = offset + length
        if kind == "rows":
            result.append(section.reshape((count * shape[0],) + tuple(shape[1:])))
        elif kind == "cols":
            result.append(
                section.reshape(count, shape[0], shape[1])
                .transpose(1, 0, 2)
                .reshape(shape[0], count * shape[1])
            )
        else:
            result.append(section.reshape(count * shape[0]))
    return tuple(result)


def pack_blocks(grads, count):
    pieces = []
    for grad, kind in zip(grads, section_kinds):
        if kind == "cols":
            pieces.append(
                grad.reshape(grad.shape[0], count, -1).transpose(1, 0, 2).reshape(count, -1)
            )
        else:
            pieces.append(grad.reshape(count, -1))
    return jnp.concatenate(pieces, axis=1)


def unpack_owned(owned_row, shapes):
    result = []
    offset = 0
    for shape in shapes:
        length = 1
        for extent in shape:
            length = length * extent
        result.append(owned_row[0, offset : offset + length].reshape(shape))
        offset = offset + length
    return tuple(result)


def collect(w_qkv, w_out, w_up, w_down, gains, up_shift, shifts):
    pieces = (w_qkv, w_out, w_up, w_down, gains, up_shift, shifts)
    shapes = [piece.shape for piece in pieces]
    owned_row = pack_owned(pieces)
    gathered = lax.all_gather(owned_row, ("dp", "fsdp"), axis=0, tiled=True)
    return unpack_whole(gathered, shapes)


def spread_grads(grads, shapes):
    count = lax.axis_size("dp") * lax.axis_size("fsdp")
    blocks = pack_blocks(grads, count)
    owned_row = lax.psum_scatter(blocks, ("dp", "fsdp"), scatter_dimension=0, tiled=True)
    return unpack_owned(owned_row, shapes)


def split_heads(qkv_rows, clips, slots):
    parts = qkv_rows.reshape(clips, slots, 3, HEADS, HEAD_WIDTH)
    return (parts[:, :, 0], parts[:, :, 1], parts[:, :, 2])


def masked_scores(query_matrix, key_matrix, valid):
    attention_scores = jnp.einsum(
        "clhd,cmhd->chlm", query_matrix, key_matrix, preferred_element_type=jnp.float32
    ) * HEAD_WIDTH ** (-0.5)
    return jnp.where(valid[:, None, None, :], attention_scores, -1e30)


def forward_layer(residual, matrices, valid, clips, slots):
    w_qkv, w_out, w_up, w_down, gains_low, up_low, shifts_low = matrices
    gains = gains_low.astype(jnp.float32)
    shifts = shifts_low.astype(jnp.float32)
    normed = layer_norm(residual, gains[0], shifts[4]).astype(jnp.bfloat16)
    qkv_bias = jnp.concatenate([shifts[0], jnp.zeros_like(shifts[0]), shifts[1]])
    qkv_rows = (jnp.dot(normed, w_qkv, preferred_element_type=jnp.float32) + qkv_bias).astype(
        jnp.bfloat16
    )
    query_matrix, key_matrix, value_matrix = split_heads(qkv_rows, clips, slots)
    masked = masked_scores(query_matrix, key_matrix, valid)
    peak = jnp.max(masked, axis=-1, keepdims=True)
    expo = jnp.exp(masked - peak)
    total = jnp.sum(expo, axis=-1, keepdims=True)
    attention_probabilities = (expo / total).astype(jnp.bfloat16)
    log_total = peak + jnp.log(total)
    mixed = jnp.einsum(
        "chlm,cmhd->clhd", attention_probabilities, value_matrix, preferred_element_type=jnp.float32
    )
    mixed = mixed.reshape(clips * slots, residual.shape[1]).astype(jnp.bfloat16)
    middle = residual + (jnp.dot(mixed, w_out, preferred_element_type=jnp.float32) + shifts[2])
    normed_two = layer_norm(middle, gains[1], shifts[5]).astype(jnp.bfloat16)
    hidden_pre = jnp.dot(normed_two, w_up, preferred_element_type=jnp.float32) + up_low.astype(
        jnp.float32
    )
    hidden = gelu_exact(hidden_pre).astype(jnp.bfloat16)
    result = middle + (jnp.dot(hidden, w_down, preferred_element_type=jnp.float32) + shifts[3])
    return (
        result,
        (residual, normed, qkv_rows, log_total, mixed, middle, normed_two, hidden_pre, hidden),
    )


def backward_layer(grad_result, matrices, record, valid, clips, slots):
    w_qkv, w_out, w_up, w_down, gains_low, up_low, shifts_low = matrices
    gains = gains_low.astype(jnp.float32)
    shifts = shifts_low.astype(jnp.float32)
    residual, normed, qkv_rows, log_total, mixed, middle, normed_two, hidden_pre, hidden = record
    width = residual.shape[1]
    down_low = grad_result.astype(jnp.bfloat16)
    grad_down = jnp.einsum("tf,td->fd", hidden, down_low, preferred_element_type=jnp.float32)
    grad_down_bias = jnp.sum(down_low, axis=0, dtype=jnp.float32)
    grad_hidden = jnp.einsum("td,fd->tf", down_low, w_down, preferred_element_type=jnp.float32)
    unused, gelu_pull = jax.vjp(gelu_exact, hidden_pre)
    grad_pre = gelu_pull(grad_hidden)[0].astype(jnp.bfloat16)
    grad_up = jnp.einsum("td,tf->df", normed_two, grad_pre, preferred_element_type=jnp.float32)
    grad_up_bias = jnp.sum(grad_pre, axis=0, dtype=jnp.float32)
    grad_normed_two = jnp.einsum("tf,df->td", grad_pre, w_up, preferred_element_type=jnp.float32)
    unused_two, norm_pull_two = jax.vjp(layer_norm, middle, gains[1], shifts[5])
    grad_mid_part, grad_gain_two, grad_shift_two = norm_pull_two(grad_normed_two)
    grad_middle = grad_result + grad_mid_part
    branch_low = grad_middle.astype(jnp.bfloat16)
    grad_out_weight = jnp.einsum("te,td->ed", mixed, branch_low, preferred_element_type=jnp.float32)
    grad_out_bias = jnp.sum(branch_low, axis=0, dtype=jnp.float32)
    grad_mixed = jnp.einsum(
        "td,ed->te", branch_low, w_out, preferred_element_type=jnp.float32
    ).astype(jnp.bfloat16)
    query_matrix, key_matrix, value_matrix = split_heads(qkv_rows, clips, slots)
    masked = masked_scores(query_matrix, key_matrix, valid)
    attention_probabilities = jnp.exp(masked - log_total)
    grad_heads = grad_mixed.reshape(clips, slots, HEADS, HEAD_WIDTH)
    grad_probs = jnp.einsum(
        "clhd,cmhd->chlm", grad_heads, value_matrix, preferred_element_type=jnp.float32
    )
    grad_values = jnp.einsum(
        "chlm,clhd->cmhd",
        attention_probabilities.astype(jnp.bfloat16),
        grad_heads,
        preferred_element_type=jnp.float32,
    )
    row_terms = jnp.sum(attention_probabilities * grad_probs, axis=-1, keepdims=True)
    grad_scores = (attention_probabilities * (grad_probs - row_terms)).astype(jnp.bfloat16)
    grad_queries = jnp.einsum(
        "chlm,cmhd->clhd", grad_scores, key_matrix, preferred_element_type=jnp.float32
    ) * HEAD_WIDTH ** (-0.5)
    grad_keys = jnp.einsum(
        "chlm,clhd->cmhd", grad_scores, query_matrix, preferred_element_type=jnp.float32
    ) * HEAD_WIDTH ** (-0.5)
    grad_qkv_rows = (
        jnp.stack([grad_queries, grad_keys, grad_values], axis=2)
        .reshape(clips * slots, 3 * width)
        .astype(jnp.bfloat16)
    )
    grad_qkv = jnp.einsum("td,te->de", normed, grad_qkv_rows, preferred_element_type=jnp.float32)
    grad_query_bias = jnp.sum(grad_qkv_rows[:, :width], axis=0, dtype=jnp.float32)
    grad_value_bias = jnp.sum(grad_qkv_rows[:, 2 * width :], axis=0, dtype=jnp.float32)
    grad_normed = jnp.einsum("te,de->td", grad_qkv_rows, w_qkv, preferred_element_type=jnp.float32)
    unused_one, norm_pull_one = jax.vjp(layer_norm, residual, gains[0], shifts[4])
    grad_res_part, grad_gain_one, grad_shift_one = norm_pull_one(grad_normed)
    grad_input = grad_middle + grad_res_part
    grad_gains = jnp.stack([grad_gain_one, grad_gain_two])
    grad_shifts = jnp.stack(
        [
            grad_query_bias,
            grad_value_bias,
            grad_out_bias,
            grad_down_bias,
            grad_shift_one,
            grad_shift_two,
        ]
    )
    return (
        grad_input,
        (grad_qkv, grad_out_weight, grad_up, grad_down, grad_gains, grad_up_bias, grad_shifts),
    )


def local(
    hidden_in,
    cotangent,
    lengths,
    qkv_weight,
    out_weight,
    up_weight,
    down_weight,
    norm_gains,
    biases,
    up_bias,
):
    clips, slots, width = hidden_in.shape
    layers = qkv_weight.shape[0]
    valid = lax.broadcasted_iota(jnp.int32, (clips, slots), 1) < lengths[:, None]
    owned_shapes = [
        qkv_weight.shape[1:],
        out_weight.shape[1:],
        up_weight.shape[1:],
        down_weight.shape[1:],
        norm_gains.shape[1:],
        up_bias.shape[1:],
        biases.shape[1:],
    ]

    def fetch(layer_index):
        return collect(
            qkv_weight[layer_index].astype(jnp.bfloat16),
            out_weight[layer_index].astype(jnp.bfloat16),
            up_weight[layer_index].astype(jnp.bfloat16),
            down_weight[layer_index].astype(jnp.bfloat16),
            norm_gains[layer_index].astype(jnp.bfloat16),
            up_bias[layer_index].astype(jnp.bfloat16),
            biases[layer_index].astype(jnp.bfloat16),
        )

    residual = hidden_in.reshape(clips * slots, width)
    kept_matrices = []
    records = []
    for layer_index in range(layers):
        matrices = fetch(layer_index)
        residual, record = forward_layer(residual, matrices, valid, clips, slots)
        kept_matrices.append(matrices)
        records.append(record)
    result = residual.reshape(clips, slots, width)
    grad_rows = cotangent.reshape(clips * slots, width)
    owned_grads = [None] * layers
    for layer_index in reversed(range(layers)):
        matrices = fetch(layer_index)
        grad_rows, terms = backward_layer(
            grad_rows, matrices, records[layer_index], valid, clips, slots
        )
        owned_grads[layer_index] = spread_grads(terms, owned_shapes)

    def stacked(member):
        return jnp.stack([owned_grads[layer_index][member] for layer_index in range(layers)])

    return (
        result,
        grad_rows.reshape(clips, slots, width),
        stacked(0),
        stacked(1),
        stacked(2),
        stacked(3),
        stacked(4),
        stacked(6),
        stacked(5),
    )


def solution(mesh):
    return jax.shard_map(
        local,
        mesh=mesh,
        in_specs=(
            P(("dp", "fsdp"), None, None),
            P(("dp", "fsdp"), None, None),
            P(("dp", "fsdp")),
            P(None, ("dp", "fsdp"), None),
            P(None, ("dp", "fsdp"), None),
            P(None, ("dp", "fsdp"), None),
            P(None, None, ("dp", "fsdp")),
            P(None, None, ("dp", "fsdp")),
            P(None, None, ("dp", "fsdp")),
            P(None, ("dp", "fsdp")),
        ),
        out_specs=(
            P(("dp", "fsdp"), None, None),
            P(("dp", "fsdp"), None, None),
            P(None, ("dp", "fsdp"), None),
            P(None, ("dp", "fsdp"), None),
            P(None, ("dp", "fsdp"), None),
            P(None, None, ("dp", "fsdp")),
            P(None, None, ("dp", "fsdp")),
            P(None, None, ("dp", "fsdp")),
            P(None, ("dp", "fsdp")),
        ),
        check_vma=False,
    )
```

profile of v0, /device:TPU:0, one launch (start us, length us, event | category | flops | bytes accessed | tf_op | source)
XLA Modules:
  0.0 1921.5 jit_solution(10509792829952141196)
XLA Ops:
  25.8 2.8 convert_element_type.422
  45.8 148.9 %all-gather.5.cloned.1.call-done = bf16[32,1,221472]{2,1,0:T(2,128)(2,1)} async-done(((bf16[1,1,221472]{2,1,0:T(2,128)(2,1)}), bf16[32,1,221472]{2,1,0:T(2,128)(2,1)}) %all-gather.5.cloned.1.call-update) | async-done | bytes 14174224 | tf_op jit(solution)/shard_map/all_gather | solution.py:77
  194.7 15.4 copy.165
  216.2 8.1 fusion.78
  224.2 142.1 %all-gather.7.cloned.1.call-done = bf16[32,1,221472]{2,1,0:T(2,128)(2,1)} async-done(((bf16[1,1,221472]{2,1,0:T(2,128)(2,1)}), bf16[32,1,221472]{2,1,0:T(2,128)(2,1)}) %all-gather.7.cloned.1.call-update) | async-done | bytes 14174224 | tf_op jit(solution)/shard_map/all_gather | solution.py:77
  366.3 15.0 copy.164
  387.9 8.0 fusion.77
  401.5 3.1 reshape.862
  411.3 6.0 fusion.31
  417.3 3.0 copy.100
  420.3 3.0 fusion.86
  428.6 3.1 fusion.41
  435.9 6.2 reshape.868
  446.6 55.6 %reshape.869 = bf16[32,3072,24]{2,1,0:T(8,128)(2,1)} reshape(bf16[32,73728]{1,0:T(8,128)(2,1)} %get-tuple-element.73) | data formatting | bytes 9437184 | tf_op jit(solution)/shard_map/reshape | solution.py:40
  502.1 20.0 %copy.105 = bf16[3072,32,24]{0,2,1:T(8,128)(2,1)} copy(bf16[3072,32,24]{2,0,1:T(8,128)(2,1)} %bitcast.250) | data formatting | bytes 9437184 | tf_op jit(solution)/shard_map/transpose | solution.py:41
  522.1 3.2 reshape.871
  527.8 20.6 %multiply_convert_fusion.3 = (bf16[496,3072]{1,0:T(8,128)(2,1)S(1)}, f32[496,3072]{1,0:T(8,128)}, f32[496,3072]{1,0:T(8,128)}) fusion(f32[3072]{0:T(1024)} %reshape.900, bf16[768,3072]{1,0:T(8,128)(2,1)} %reshape.868, f32[496,768]{1,0:T(8,128)} %copy-done.27, f32[768]{0:T(1024)} %add.213, f32[768]{0:T(1024)} %mul.380, f32[496]{0:T(512)} %fusion.53, ...), kind=kOutput, calls=%fused_computation.51 | convolution fusion | flops 2442891264 | bytes 21501824 | tf_op jit(solution)/shard_map/dot_general | solution.py:122
  548.4 2.7 fusion.88
  552.2 3.6 fusion.32
  555.8 3.0 copy.114
  558.8 3.0 fusion.89
  566.2 3.1 fusion.40
  572.8 6.2 reshape.877
  582.1 55.6 %reshape.878 = bf16[32,3072,24]{2,1,0:T(8,128)(2,1)} reshape(bf16[32,73728]{1,0:T(8,128)(2,1)} %get-tuple-element.71) | data formatting | bytes 9437184 | tf_op jit(solution)/shard_map/reshape | solution.py:40
  637.7 19.9 %copy.119 = bf16[3072,32,24]{0,2,1:T(8,128)(2,1)} copy(bf16[3072,32,24]{2,0,1:T(8,128)(2,1)} %bitcast.251) | data formatting | bytes 9437184 | tf_op jit(solution)/shard_map/transpose | solution.py:41
  657.5 18.4 multiply_convert_fusion.2
  676.0 5.3 convert_reduce_fusion
  681.3 6.9 multiply_reduce_fusion.2
  692.1 7.5 fusion.34
  699.5 6.3 multiply_reduce_fusion.1
  705.9 3.8 multiply_convert_fusion.1
  709.7 3.2 multiply_bitcast_fusion.2
  721.3 8.0 convert_reduce_fusion.1
  729.4 3.4 multiply_reduce_fusion.4
  736.7 7.5 fusion.37
  744.1 6.3 multiply_reduce_fusion
  750.5 3.7 multiply_convert_fusion
  754.2 3.2 multiply_bitcast_fusion
  759.6 5.3 fusion.67
  767.1 5.5 fusion.68
  775.1 4.0 multiply_reduce_fusion.5
  779.1 5.3 fusion.62
  786.7 5.9 fusion.65
  792.6 5.1 fusion.91
  798.0 6.6 reshape.893
  804.6 6.4 constant_dynamic-update-slice_fusion.27
  812.8 8.1 reshape.895
  821.0 6.9 convolution_bitcast_fusion
  827.8 25.7 %copy.136 = f32[32,3072,24]{2,1,0:T(8,128)} copy(f32[32,3072,24]{1,0,2:T(8,128)} %convolution_bitcast_fusion) | data formatting | bytes 18874368 | tf_op jit(solution)/shard_map/transpose | solution.py:54
  853.6 70.8 %reshape.896 = f32[32,73728]{1,0:T(8,128)} reshape(f32[32,3072,24]{2,1,0:T(8,128)} %copy.136) | data formatting | bytes 18874368 | tf_op jit(solution)/shard_map/reshape | solution.py:54
  925.6 6.6 reshape.885
  932.2 6.3 constant_dynamic-update-slice_fusion.17
  938.4 2.8 reshape.886
  941.3 8.1 reshape.887
  949.4 25.7 %copy.129 = f32[3072,32,24]{2,0,1:T(8,128)} copy(f32[3072,32,24]{0,2,1:T(8,128)} %bitcast.278) | data formatting | bytes 18874368 | tf_op jit(solution)/shard_map/reshape | solution.py:54
  975.1 71.1 %reshape.889 = f32[32,73728]{1,0:T(8,128)} reshape(f32[32,3072,24]{2,1,0:T(8,128)} %bitcast.249) | data formatting | bytes 18874368 | tf_op jit(solution)/shard_map/reshape | solution.py:54
  1049.0 8.5 constant_dynamic-update-slice_fusion.25
  1057.5 4.1 constant_dynamic-update-slice_fusion.24
  1067.6 8.4 constant_dynamic-update-slice_fusion.15
  1076.0 4.2 constant_dynamic-update-slice_fusion.14
  1089.7 6.2 add_bitcast_fusion.1
  1095.9 795.2 %all-reduce.5.cloned.1.call-done = (f32[32,221472]{1,0:T(8,128)}, f32[32,221472]{1,0:T(8,128)}) async-done(((f32[32,221472]{1,0:T(8,128)}, f32[32,221472]{1,0:T(8,128)}), (f32[32,221472]{1,0:T(8,128)}, f32[32,221472]{1,0:T(8,128)})) %all-reduce.5.cloned.1.call-update) | async-done | bytes 56696848
  1891.1 3.2 dynamic-slice_reduce_fusion.4
  1897.7 7.2 dynamic-slice_reduce_fusion
  (513 shorter events, 147.0 us)
Async XLA Ops:
  7.2 7.8 copy-start.111
  7.2 7.9 copy-start.112
  7.2 7.9 copy-start.95
  7.2 187.5 %all-gather.5.cloned.1.call-start = ((), (), s32[]{:S(2)}) async-start(), calls=%async_computation | async-start | bytes 29246976 | tf_op jit(solution)/shard_map/all_gather | solution.py:77
  13.9 26.1 %copy-start.22 = (f32[1,496,768]{2,1,0:T(8,128)S(1)}, f32[1,496,768]{2,1,0:T(8,128)}, u32[]{:S(2)}) copy-start(f32[1,496,768]{2,1,0:T(8,128)} %param.11) | copy-start | bytes 4571140
  21.9 344.5 %all-gather.7.cloned.1.call-start = ((), (), s32[]{:S(2)}) async-start(), calls=%async_computation.1 | async-start | bytes 29246976 | tf_op jit(solution)/shard_map/all_gather | solution.py:77
  21.9 21.4 %copy-start.15 = (f32[1,496,768]{2,1,0:T(8,128)S(1)}, f32[1,496,768]{2,1,0:T(8,128)}, u32[]{:S(2)}) copy-start(f32[1,496,768]{2,1,0:T(8,128)} %param.10) | copy-start | bytes 4571140
  39.2 1851.9 %all-reduce.5.cloned.1.call-start = ((), (), s32[]{:S(2)}) async-start(), calls=%async_computation.2 | async-start | bytes 113442816
  381.4 6.4 copy-start.3
  411.3 9.0 copy-start.108
  435.9 7.0 copy-start.62
  435.9 7.7 copy-start.16
  435.9 7.7 copy-start.44
  435.9 7.7 copy-start.47
  435.9 7.7 copy-start.105
  502.1 20.0 %copy-start.11 = (bf16[32,55296]{1,0:T(8,128)(2,1)S(1)}, bf16[32,55296]{1,0:T(8,128)(2,1)}, u32[]{:S(2)}) copy-start(bf16[32,55296]{1,0:T(8,128)(2,1)} %slice.370) | copy-start | bytes 10616836
  526.2 25.3 %copy-start.100 = (f32[768]{0:T(1024)}, f32[768]{0:T(1024)S(1)}, u32[]{:S(2)}) copy-start(f32[768]{0:T(1024)S(1)} %add.223) | copy-start | bytes 9220
  527.7 23.7 %copy-start.82 = (f32[768]{0:T(1024)}, f32[768]{0:T(1024)S(1)}, u32[]{:S(2)}) copy-start(f32[768]{0:T(1024)S(1)} %mul.389) | copy-start | bytes 9220
  527.7 20.6 %copy-start.28 = (f32[496,768]{1,0:T(8,128)S(1)}, f32[496,768]{1,0:T(8,128)}, u32[]{:S(2)}) copy-start(f32[496,768]{1,0:T(8,128)} %copy-done.27) | copy-start | bytes 4571140
  527.7 20.6 %copy-start.36 = (bf16[3072,32,24]{0,2,1:T(8,128)(2,1)S(1)}, bf16[3072,32,24]{0,2,1:T(8,128)(2,1)}, u32[]{:S(2)}) copy-start(bf16[3072,32,24]{0,2,1:T(8,128)(2,1)} %copy.105) | copy-start | bytes 14155780
  527.8 20.6 %copy-start.106 = (f32[768]{0:T(1024)S(1)}, f32[768]{0:T(1024)}, u32[]{:S(2)}) copy-start(f32[768]{0:T(1024)} %add.218) | copy-start | bytes 9220
  552.2 6.6 copy-start.109
  572.8 6.5 copy-start.32
  572.8 6.5 copy-start.107
  581.8 106.4 %copy-start.24 = (f32[496,768]{1,0:T(8,128)}, f32[496,768]{1,0:T(8,128)S(1)}, u32[]{:S(2)}) copy-start(f32[496,768]{1,0:T(8,128)S(1)} %get-tuple-element.116) | copy-start | bytes 4571140
  657.5 18.4 copy-start.23
  657.5 18.4 copy-start.35
  681.3 6.9 copy-start.115
  692.0 13.8 slice-start.3
  692.1 13.8 slice-start.4
  714.5 6.6 slice-start.12
  714.6 6.6 slice-start.16
  719.0 10.3 slice-start.14
  721.2 8.1 copy-start.51
  721.2 8.1 copy-start.29
  721.2 8.1 slice-start.15
  721.2 8.1 copy-start.67
  721.2 8.1 copy-start.80
  721.2 8.1 copy-start.92
  736.6 13.8 slice-start
  736.6 13.8 slice-start.1
  759.6 7.5 copy-start.25
  759.6 7.5 copy-start.116
  779.0 7.6 copy-start.30
  779.1 7.6 copy-start.98
  779.1 7.6 copy-start.118
  812.8 8.1 copy-start.50
  853.5 70.9 %copy-start.103 = (f32[768]{0:T(1024)S(1)}, f32[768]{0:T(1024)}, u32[]{:S(2)}) copy-start(f32[768]{0:T(1024)} %get-tuple-element.37) | copy-start | bytes 9220
  853.5 71.2 %copy-start.86 = (f32[3072]{0:T(1024)S(1)}, f32[3072]{0:T(1024)}, u32[]{:S(2)}) copy-start(f32[3072]{0:T(1024)} %get-tuple-element.126) | copy-start | bytes 36868
  853.5 71.5 %copy-start.85 = (f32[768]{0:T(1024)S(1)}, f32[768]{0:T(1024)}, u32[]{:S(2)}) copy-start(f32[768]{0:T(1024)} %get-tuple-element.57) | copy-start | bytes 9220
  853.5 71.6 %copy-start.84 = (f32[768]{0:T(1024)S(1)}, f32[768]{0:T(1024)}, u32[]{:S(2)}) copy-start(f32[768]{0:T(1024)} %get-tuple-element.75) | copy-start | bytes 9220
  853.5 71.7 %copy-start.99 = (f32[768]{0:T(1024)S(1)}, f32[768]{0:T(1024)}, u32[]{:S(2)}) copy-start(f32[768]{0:T(1024)} %get-tuple-element.45) | copy-start | bytes 9220
  975.1 71.1 %copy-start.104 = (f32[768]{0:T(1024)S(1)}, f32[768]{0:T(1024)}, u32[]{:S(2)}) copy-start(f32[768]{0:T(1024)} %get-tuple-element.33) | copy-start | bytes 9220
  975.1 71.4 %copy-start.88 = (f32[3072]{0:T(1024)S(1)}, f32[3072]{0:T(1024)}, u32[]{:S(2)}) copy-start(f32[3072]{0:T(1024)} %get-tuple-element.55) | copy-start | bytes 36868
  975.1 71.7 %copy-start.76 = (f32[768]{0:T(1024)S(1)}, f32[768]{0:T(1024)}, u32[]{:S(2)}) copy-start(f32[768]{0:T(1024)} %get-tuple-element.53) | copy-start | bytes 9220
  975.1 71.8 %copy-start.81 = (f32[768]{0:T(1024)S(1)}, f32[768]{0:T(1024)}, u32[]{:S(2)}) copy-start(f32[768]{0:T(1024)} %get-tuple-element.51) | copy-start | bytes 9220
  975.1 72.0 %copy-start.102 = (f32[768]{0:T(1024)S(1)}, f32[768]{0:T(1024)}, u32[]{:S(2)}) copy-start(f32[768]{0:T(1024)} %get-tuple-element.43) | copy-start | bytes 9220
  1047.4 10.0 slice-start.6
  1049.0 8.5 slice-start.7
  1049.0 8.5 slice-start.8
  1057.5 8.5 copy-start.19
  1066.0 10.0 slice-start.9
  1067.6 8.4 slice-start.10
  1067.6 8.4 slice-start.11
  (77 other events, 230.2 us)
Sparse Core Ops, SparseCore 0:
  22.0 172.6 all-gather.4
  198.2 168.1 all-gather.6
  1084.7 806.3 all-reduce.4
where the time goes:
time: 1930 us; the launch traced here: 1920 us
  waiting for transfers between devices  1090 us (56%)
  local copies, waits for them, and re-layouts  599 us (31%)
  matrix products  179 us (9%)
  other arithmetic  40.2 us (2%)
    unnamed x4, waiting for transfers between devices  795 us
    all_gather x2, waiting for transfers between devices, collect(): gathered = lax.all_gather(owned_row, ('dp', 'fsdp'), axis=0, tiled=True)  291 us
    reshape x7, local copies, waits for them, and re-layouts, pack_blocks(): grad.reshape(grad.shape[0], count, -1).transpose(1, 0, 2).reshape(count, -1)  168 us
    unnamed x322, local copies, waits for them, and re-layouts  114 us
    reshape x2, local copies, waits for them, and re-layouts, unpack_whole(): section.reshape(count, shape[0], shape[1]).transpose(1, 0, 2)  111 us
    transpose x2, local copies, waits for them, and re-layouts, unpack_whole(): result.append(section.reshape(count, shape[0], shape[1]).transpose(1, 0,...  39.8 us
    dot_general x2, matrix products, forward_layer(): jnp.dot(normed_two, w_up, preferred_element_type=jnp.float32)  39 us
  transfers between devices with their start and end apart: 3, of which 3 were waited for; matrix products, arithmetic and copies ran while one was open for 3% of the time, Pallas kernels for 0%

commit v1 on v0

--- a/solution.py
+++ b/solution.py
@@ -74,7 +74,14 @@
     pieces = (w_qkv, w_out, w_up, w_down, gains, up_shift, shifts)
     shapes = [piece.shape for piece in pieces]
     owned_row = pack_owned(pieces)
-    gathered = lax.all_gather(owned_row, ("dp", "fsdp"), axis=0, tiled=True)
+    ways, here = (lax.axis_size(("dp", "fsdp")), lax.axis_index(("dp", "fsdp")))
+    gathered, reach = (owned_row, 1)
+    while reach < ways:
+        theirs = lax.ppermute(gathered, ("dp", "fsdp"), [(d, d ^ reach) for d in range(ways)])
+        mine_first = jnp.concatenate([gathered, theirs], axis=0)
+        theirs_first = jnp.concatenate([theirs, gathered], axis=0)
+        gathered = jnp.where(here & reach == 0, mine_first, theirs_first)
+        reach = 2 * reach
     return unpack_whole(gathered, shapes)
 
 

time: 1930 us -> 2370 us (1.23)
  waiting for transfers between devices: 1090 us -> 1490 us
  other arithmetic: 40.2 us -> 101 us
  local copies, waits for them, and re-layouts: 599 us -> 569 us
    ppermute x0 -> x10, waiting for transfers between devices: none -> 691 us  [collect(): lax.ppermute(gathered, ('dp', 'fsdp'), [(d, d ^ reach) for d in range(way...]
    all_gather x2 -> x0, waiting for transfers between devices: 291 us -> none  [collect(): gathered = lax.all_gather(owned_row, ('dp', 'fsdp'), axis=0, tiled=True)]
    select_n x0 -> x10, other arithmetic: none -> 57 us  [collect(): gathered = jnp.where(here & reach == 0, mine_first, theirs_first)]
    unnamed x322 -> x314, local copies, waits for them, and re-layouts: 114 us -> 88.2 us
    unnamed x4 -> x2, waiting for transfers between devices: 795 us -> 796 us
  transfers between devices with their start and end apart: 3 -> 11, of which waited for: 3 -> 9; matrix products, arithmetic and copies ran while one was open for 3% -> 4% of each run, Pallas kernels for 0% -> 0%
where the time goes in v1:
time: 2370 us; the launch traced here: 2360 us
  waiting for transfers between devices  1490 us (63%)
  local copies, waits for them, and re-layouts  569 us (24%)
  matrix products  174 us (7%)
  other arithmetic  101 us (4%)
    unnamed x2, waiting for transfers between devices  796 us
    ppermute x10, waiting for transfers between devices, collect(): lax.ppermute(gathered, ('dp', 'fsdp'), [(d, d ^ reach) for d in range(way...  691 us
    reshape x7, local copies, waits for them, and re-layouts, pack_blocks(): grad.reshape(grad.shape[0], count, -1).transpose(1, 0, 2).reshape(count, -1)  168 us
    reshape x2, local copies, waits for them, and re-layouts, unpack_whole(): section.reshape(count, shape[0], shape[1]).transpose(1, 0, 2)  111 us
    unnamed x314, local copies, waits for them, and re-layouts  88.2 us
    select_n x10, other arithmetic, collect(): gathered = jnp.where(here & reach == 0, mine_first, theirs_first)  57 us
  transfers between devices with their start and end apart: 11, of which 9 were waited for; matrix products, arithmetic and copies ran while one was open for 4% of the time, Pallas kernels for 0%

profile of v1, /device:TPU:0, one launch (start us, length us, event | category | flops | bytes accessed | tf_op | source)
XLA Modules:
  0.0 2364.0 jit_solution(7050424908374398852)
XLA Ops:
  51.5 7.3 broadcast_select_fusion.1
  61.8 6.6 broadcast_select_fusion
  68.5 13.8 collective-permute-done.1
  82.3 5.0 maximum_select_fusion.6
  89.4 11.2 collective-permute-done.6
  100.6 4.8 maximum_select_fusion.7
  107.3 21.7 collective-permute-done.2
  129.0 4.7 maximum_select_fusion.4
  135.9 28.9 %collective-permute-done.7 = bf16[4,221472]{1,0:T(4,128)(2,1)S(1)} collective-permute-done((bf16[4,221472]{1,0:T(4,128)(2,1)S(1)}, bf16[4,221472]{1,0:T(4,128)(2,1)S(1)}, u32[]{:S(2)}, u32[]{:S(2)}) %collective-permute-start.7) | collective-permute-done | bytes 1771808 | tf_op jit(solution)/shard_map/ppermute | solution.py:80
  164.8 4.7 maximum_select_fusion.5
  171.1 117.2 %collective-permute-done.3 = bf16[8,221472]{1,0:T(8,128)(2,1)S(1)} collective-permute-done((bf16[8,221472]{1,0:T(8,128)(2,1)S(1)}, bf16[8,221472]{1,0:T(8,128)(2,1)S(1)}, u32[]{:S(2)}, u32[]{:S(2)}) %collective-permute-start.3) | collective-permute-done | bytes 3543584 | tf_op jit(solution)/shard_map/ppermute | solution.py:80
  290.6 3.4 collective-permute-start.4
  294.0 66.1 %collective-permute-done.8 = bf16[8,221472]{1,0:T(8,128)(2,1)S(1)} collective-permute-done((bf16[8,221472]{1,0:T(8,128)(2,1)S(1)}, bf16[8,221472]{1,0:T(8,128)(2,1)S(1)}, u32[]{:S(2)}, u32[]{:S(2)}) %collective-permute-start.8) | collective-permute-done | bytes 3543584 | tf_op jit(solution)/shard_map/ppermute | solution.py:80
  363.5 377.6 %collective-permute-done.4 = bf16[16,221472]{1,0:T(8,128)(2,1)S(1)} collective-permute-done((bf16[16,221472]{1,0:T(8,128)(2,1)S(1)}, bf16[16,221472]{1,0:T(8,128)(2,1)S(1)}, u32[]{:S(2)}, u32[]{:S(2)}) %collective-permute-start.4) | collective-permute-done | bytes 7087136 | tf_op jit(solution)/shard_map/ppermute | solution.py:80
  741.1 9.3 maximum_select_fusion
  750.4 8.0 fusion.78
  762.5 54.8 %collective-permute-done.9 = bf16[16,221472]{1,0:T(8,128)(2,1)} collective-permute-done((bf16[16,221472]{1,0:T(8,128)(2,1)S(1)}, bf16[16,221472]{1,0:T(8,128)(2,1)}, u32[]{:S(2)}, u32[]{:S(2)}) %collective-permute-start.9) | collective-permute-done | bytes 7087136 | tf_op jit(solution)/shard_map/ppermute | solution.py:80
  817.2 9.8 maximum_select_fusion.1
  832.1 8.2 fusion.77
  855.7 5.9 fusion.31
  879.5 6.2 reshape.868
  890.1 55.3 %reshape.869 = bf16[32,3072,24]{2,1,0:T(8,128)(2,1)} reshape(bf16[32,73728]{1,0:T(8,128)(2,1)} %get-tuple-element.73) | data formatting | bytes 9437184 | tf_op jit(solution)/shard_map/reshape | solution.py:40
  945.4 20.0 copy.105
  965.4 3.4 reshape.871
  971.2 20.5 multiply_convert_fusion.3
  995.6 3.5 fusion.32
  1014.9 6.4 reshape.877
  1024.4 55.5 %reshape.878 = bf16[32,3072,24]{2,1,0:T(8,128)(2,1)} reshape(bf16[32,73728]{1,0:T(8,128)(2,1)} %get-tuple-element.71) | data formatting | bytes 9437184 | tf_op jit(solution)/shard_map/reshape | solution.py:40
  1079.9 19.8 copy.119
  1099.7 18.5 multiply_convert_fusion.2
  1118.2 5.3 convert_reduce_fusion
  1123.5 6.9 multiply_reduce_fusion.2
  1134.2 7.5 fusion.34
  1141.6 6.3 multiply_reduce_fusion.1
  1148.0 3.7 multiply_convert_fusion.1
  1166.4 3.6 convert_reduce_fusion.1
  1170.1 3.5 multiply_reduce_fusion.4
  1177.4 7.5 fusion.37
  1184.9 6.3 multiply_reduce_fusion
  1191.3 4.0 multiply_convert_fusion
  1200.6 5.3 fusion.67
  1208.2 5.5 fusion.68
  1216.1 4.0 multiply_reduce_fusion.5
  1220.2 5.3 fusion.62
  1227.7 5.7 fusion.65
  1233.4 5.1 fusion.92
  1238.8 6.6 reshape.893
  1245.4 6.4 constant_dynamic-update-slice_fusion.27
  1253.6 8.1 reshape.895
  1261.7 6.9 convolution_bitcast_fusion
  1268.6 25.8 %copy.136 = f32[32,3072,24]{2,1,0:T(8,128)} copy(f32[32,3072,24]{1,0,2:T(8,128)} %convolution_bitcast_fusion) | data formatting | bytes 18874368 | tf_op jit(solution)/shard_map/transpose | solution.py:54
  1294.4 70.9 %reshape.896 = f32[32,73728]{1,0:T(8,128)} reshape(f32[32,3072,24]{2,1,0:T(8,128)} %copy.136) | data formatting | bytes 18874368 | tf_op jit(solution)/shard_map/reshape | solution.py:54
  1366.4 6.6 reshape.885
  1373.0 6.3 constant_dynamic-update-slice_fusion.17
  1382.2 8.1 reshape.887
  1390.3 25.7 %copy.129 = f32[3072,32,24]{2,0,1:T(8,128)} copy(f32[3072,32,24]{0,2,1:T(8,128)} %bitcast.262) | data formatting | bytes 18874368 | tf_op jit(solution)/shard_map/reshape | solution.py:54
  1416.0 71.3 %reshape.889 = f32[32,73728]{1,0:T(8,128)} reshape(f32[32,3072,24]{2,1,0:T(8,128)} %bitcast.241) | data formatting | bytes 18874368 | tf_op jit(solution)/shard_map/reshape | solution.py:54
  1490.1 8.5 constant_dynamic-update-slice_fusion.25
  1498.7 4.1 constant_dynamic-update-slice_fusion.24
  1508.8 8.5 constant_dynamic-update-slice_fusion.15
  1517.2 4.2 constant_dynamic-update-slice_fusion.14
  1531.0 6.5 add_bitcast_fusion.1
  1537.5 795.7 %all-reduce.5.cloned.1.call-done = (f32[32,221472]{1,0:T(8,128)}, f32[32,221472]{1,0:T(8,128)}) async-done(((f32[32,221472]{1,0:T(8,128)}, f32[32,221472]{1,0:T(8,128)}), (f32[32,221472]{1,0:T(8,128)}, f32[32,221472]{1,0:T(8,128)})) %all-reduce.5.cloned.1.call-update) | async-done | bytes 56696848
  2339.8 7.2 dynamic-slice_reduce_fusion
  (535 shorter events, 206.3 us)
Async XLA Ops:
  7.2 12.8 copy-start.108
  7.2 12.9 copy-start.109
  7.2 12.9 copy-start.93
  7.2 2326.0 %all-reduce.5.cloned.1.call-start = ((), (), s32[]{:S(2)}) async-start(), calls=%async_computation | async-start | bytes 113442816
  13.0 32.9 %copy-start.14 = (f32[1,496,768]{2,1,0:T(8,128)S(1)}, f32[1,496,768]{2,1,0:T(8,128)}, u32[]{:S(2)}) copy-start(f32[1,496,768]{2,1,0:T(8,128)} %param.10) | copy-start | bytes 4571140
  15.0 31.7 %copy-start.21 = (f32[1,496,768]{2,1,0:T(8,128)S(1)}, f32[1,496,768]{2,1,0:T(8,128)}, u32[]{:S(2)}) copy-start(f32[1,496,768]{2,1,0:T(8,128)} %param.11) | copy-start | bytes 4571140
  28.9 22.5 collective-permute-start
  45.8 16.0 collective-permute-start.5
  46.1 22.4 copy-start.63
  47.7 14.1 copy-start.44
  50.9 54.6 %copy-start.70 = (f32[496]{0:T(512)}, f32[496]{0:T(512)S(1)}, u32[]{:S(2)}) copy-start(f32[496]{0:T(512)S(1)} %multiply_reduce_fusion.13) | copy-start | bytes 5956
  58.8 23.5 collective-permute-start.1
  68.4 32.2 %collective-permute-start.6 = (bf16[2,221472]{1,0:T(2,128)(2,1)S(1)}, bf16[2,221472]{1,0:T(2,128)(2,1)S(1)}, u32[]{:S(2)}, u32[]{:S(2)}) collective-permute-start(bf16[2,221472]{1,0:T(2,128)(2,1)S(1)} %broadcast_select_fusion), channel_id=1, source_target_pairs={{0,2},{1,3},{2,0},{3,1},{4,6},{5,7},{6,4},{7,5},{8,10},{9,11},{10,... | collective-permute-start | bytes 2657672 | tf_op jit(solution)/shard_map/ppermute | solution.py:80
  87.3 41.7 %collective-permute-start.2 = (bf16[4,221472]{1,0:T(4,128)(2,1)S(1)}, bf16[4,221472]{1,0:T(4,128)(2,1)S(1)}, u32[]{:S(2)}, u32[]{:S(2)}) collective-permute-start(bf16[4,221472]{1,0:T(4,128)(2,1)S(1)} %maximum_select_fusion.6), channel_id=1, source_target_pairs={{0,4},{1,5},{2,6},{3,7},{4,0},{5,1},{6,2},{7,3},{8,12},{9,13},{10,... | collective-permute-start | bytes 5315336 | tf_op jit(solution)/shard_map/ppermute | solution.py:80
  105.5 59.3 %collective-permute-start.7 = (bf16[4,221472]{1,0:T(4,128)(2,1)S(1)}, bf16[4,221472]{1,0:T(4,128)(2,1)S(1)}, u32[]{:S(2)}, u32[]{:S(2)}) collective-permute-start(bf16[4,221472]{1,0:T(4,128)(2,1)S(1)} %maximum_select_fusion.7), channel_id=1, source_target_pairs={{0,4},{1,5},{2,6},{3,7},{4,0},{5,1},{6,2},{7,3},{8,12},{9,13},{10,... | collective-permute-start | bytes 5315336 | tf_op jit(solution)/shard_map/ppermute | solution.py:80
  133.7 154.5 %collective-permute-start.3 = (bf16[8,221472]{1,0:T(8,128)(2,1)S(1)}, bf16[8,221472]{1,0:T(8,128)(2,1)S(1)}, u32[]{:S(2)}, u32[]{:S(2)}) collective-permute-start(bf16[8,221472]{1,0:T(8,128)(2,1)S(1)} %maximum_select_fusion.4), channel_id=1, source_target_pairs={{0,8},{1,9},{2,10},{3,11},{4,12},{5,13},{6,14},{7,15},{8,0},{9,1},... | collective-permute-start | bytes 10630664 | tf_op jit(solution)/shard_map/ppermute | solution.py:80
  169.5 190.6 %collective-permute-start.8 = (bf16[8,221472]{1,0:T(8,128)(2,1)S(1)}, bf16[8,221472]{1,0:T(8,128)(2,1)S(1)}, u32[]{:S(2)}, u32[]{:S(2)}) collective-permute-start(bf16[8,221472]{1,0:T(8,128)(2,1)S(1)} %maximum_select_fusion.5), channel_id=1, source_target_pairs={{0,8},{1,9},{2,10},{3,11},{4,12},{5,13},{6,14},{7,15},{8,0},{9,1},... | collective-permute-start | bytes 10630664 | tf_op jit(solution)/shard_map/ppermute | solution.py:80
  290.6 450.5 %collective-permute-start.4 = (bf16[16,221472]{1,0:T(8,128)(2,1)S(1)}, bf16[16,221472]{1,0:T(8,128)(2,1)S(1)}, u32[]{:S(2)}, u32[]{:S(2)}) collective-permute-start(bf16[16,221472]{1,0:T(8,128)(2,1)S(1)} %maximum_select_fusion.2), channel_id=1, source_target_pairs={{0,16},{1,17},{2,18},{3,19},{4,20},{5,21},{6,22},{7,23},{8,24},{9,... | collective-permute-start | bytes 21261320 | tf_op jit(solution)/shard_map/ppermute | solution.py:80
  362.5 454.8 %collective-permute-start.9 = (bf16[16,221472]{1,0:T(8,128)(2,1)S(1)}, bf16[16,221472]{1,0:T(8,128)(2,1)}, u32[]{:S(2)}, u32[]{:S(2)}) collective-permute-start(bf16[16,221472]{1,0:T(8,128)(2,1)S(1)} %maximum_select_fusion.3), channel_id=1, source_target_pairs={{0,16},{1,17},{2,18},{3,19},{4,20},{5,21},{6,22},{7,23},{8,24},{9,... | collective-permute-start | bytes 21261320 | tf_op jit(solution)/shard_map/ppermute | solution.py:80
  832.1 13.8 slice-start.8
  853.5 8.1 copy-start.94
  855.7 8.8 copy-start.105
  876.6 10.6 copy-start.45
  879.4 7.0 copy-start.62
  879.4 7.7 copy-start.15
  879.5 7.7 copy-start.48
  879.5 7.7 copy-start.103
  945.4 20.0 slice-start.6
  969.6 25.9 %copy-start.98 = (f32[768]{0:T(1024)}, f32[768]{0:T(1024)S(1)}, u32[]{:S(2)}) copy-start(f32[768]{0:T(1024)S(1)} %add.230) | copy-start | bytes 9220
  971.2 24.4 %copy-start.82 = (f32[768]{0:T(1024)}, f32[768]{0:T(1024)S(1)}, u32[]{:S(2)}) copy-start(f32[768]{0:T(1024)S(1)} %mul.396) | copy-start | bytes 9220
  971.2 20.5 copy-start.10
  971.2 20.5 copy-start.27
  971.2 20.5 copy-start.104
  1024.1 106.3 %copy-start.23 = (f32[496,768]{1,0:T(8,128)}, f32[496,768]{1,0:T(8,128)S(1)}, u32[]{:S(2)}) copy-start(f32[496,768]{1,0:T(8,128)S(1)} %get-tuple-element.116) | copy-start | bytes 4571140
  1099.7 18.5 copy-start.22
  1099.7 18.5 copy-start.34
  1123.5 6.9 copy-start.112
  1134.1 13.8 slice-start.3
  1134.2 13.8 slice-start.4
  1177.4 13.9 slice-start
  1177.4 13.9 slice-start.1
  1200.6 7.6 copy-start.24
  1200.6 7.6 copy-start.113
  1220.1 7.6 copy-start.29
  1220.1 7.6 copy-start.43
  1220.1 7.6 copy-start.96
  1253.6 8.1 copy-start.51
  1294.4 70.9 %copy-start.101 = (f32[768]{0:T(1024)S(1)}, f32[768]{0:T(1024)}, u32[]{:S(2)}) copy-start(f32[768]{0:T(1024)} %get-tuple-element.37) | copy-start | bytes 9220
  1294.4 71.2 %copy-start.86 = (f32[3072]{0:T(1024)S(1)}, f32[3072]{0:T(1024)}, u32[]{:S(2)}) copy-start(f32[3072]{0:T(1024)} %get-tuple-element.126) | copy-start | bytes 36868
  1294.4 71.5 %copy-start.85 = (f32[768]{0:T(1024)S(1)}, f32[768]{0:T(1024)}, u32[]{:S(2)}) copy-start(f32[768]{0:T(1024)} %get-tuple-element.57) | copy-start | bytes 9220
  1294.4 71.6 %copy-start.84 = (f32[768]{0:T(1024)S(1)}, f32[768]{0:T(1024)}, u32[]{:S(2)}) copy-start(f32[768]{0:T(1024)} %get-tuple-element.75) | copy-start | bytes 9220
  1294.4 71.8 %copy-start.97 = (f32[768]{0:T(1024)S(1)}, f32[768]{0:T(1024)}, u32[]{:S(2)}) copy-start(f32[768]{0:T(1024)} %get-tuple-element.45) | copy-start | bytes 9220
  1416.0 71.3 %copy-start.102 = (f32[768]{0:T(1024)S(1)}, f32[768]{0:T(1024)}, u32[]{:S(2)}) copy-start(f32[768]{0:T(1024)} %get-tuple-element.33) | copy-start | bytes 9220
  1416.0 71.7 %copy-start.57 = (f32[3072]{0:T(1024)S(1)}, f32[3072]{0:T(1024)}, u32[]{:S(2)}) copy-start(f32[3072]{0:T(1024)} %get-tuple-element.55) | copy-start | bytes 36868
  1416.0 71.9 %copy-start.76 = (f32[768]{0:T(1024)S(1)}, f32[768]{0:T(1024)}, u32[]{:S(2)}) copy-start(f32[768]{0:T(1024)} %get-tuple-element.53) | copy-start | bytes 9220
  1416.0 72.0 %copy-start.81 = (f32[768]{0:T(1024)S(1)}, f32[768]{0:T(1024)}, u32[]{:S(2)}) copy-start(f32[768]{0:T(1024)} %get-tuple-element.51) | copy-start | bytes 9220
  1416.0 72.2 %copy-start.100 = (f32[768]{0:T(1024)S(1)}, f32[768]{0:T(1024)}, u32[]{:S(2)}) copy-start(f32[768]{0:T(1024)} %get-tuple-element.43) | copy-start | bytes 9220
  1488.5 10.1 slice-start.10
  1490.1 8.5 slice-start.11
  1490.1 8.5 slice-start.12
  1498.7 8.5 copy-start.18
  1507.2 10.0 slice-start.13
  1508.8 8.5 slice-start.14
  1508.8 8.5 slice-start.15
  (86 other events, 290.1 us)
Sparse Core Ops, SparseCore 0:
  1526.0 807.2 all-reduce.4
